TPU v7x, 32 devices: a whole 2x2x4 slice. The times are simulated.
32 devices in a mesh: leaf: 8 (over y, x, core), probe: 4 (over z).
Axes of the slice: x: 2, y: 2, z: 4, core: 2. Of those that a mesh axis runs over, the one named last changes fastest.
Arguments:
- leaf_blocks: float32 [8192, 1024], P('leaf'), may hold values from -0.1875 to 0.1875
- block_mask: int32 [8, 8, 8], P('leaf'), may hold values 0 or 1
- row_factor_stack: float32 [3, 8192, 128], P(None, 'leaf'), may hold values from -0.5 to 0.5
- column_factor_stack: float32 [3, 8192, 128], P(None, 'leaf'), may hold values from -0.0625 to 0.0625
- probes: float32 [8192, 1024], P('leaf', 'probe'), may hold values from -6 to 6
Outputs:
- applied: float32 [8192, 1024], P('leaf', 'probe')
- probe_gram: float32 [1024, 1024], P('leaf', 'probe')
All inputs are finite; a program needn't handle non-finite values. No bound on the sum of `block_mask` on one device may be relied on, other than what follows from the above.
Results may differ from a plain program's by a relative error of at most 0.0001.
Values sent between devices are 32-bit elements; how exact they have to be, the bound alone decides.
A program may use at most 64 MiB of HBM per device.

v0:
```python
import jax
import jax.numpy as jnp
from jax import lax
from jax.sharding import PartitionSpec as P


def partner(value, axis, distance):
    mask = 2**distance
    pairs = [(source, source ^ mask) for source in range(lax.axis_size(axis))]
    return lax.ppermute(value, axis, pairs)


def local(leaf_blocks, block_mask, row_factor_stack, column_factor_stack, probes):
    leaf_points = leaf_blocks.shape[1]
    mask_side = block_mask.shape[1]
    block_span_width = leaf_points // mask_side
    depth = row_factor_stack.shape[0]
    weights = block_mask[0].astype(jnp.float32)
    masked = (
        leaf_blocks.reshape(mask_side, block_span_width, mask_side, block_span_width)
        * weights[:, None, :, None]
    ).reshape(leaf_points, leaf_points)
    applied = jnp.dot(
        masked, probes, precision=lax.Precision.HIGHEST, preferred_element_type=jnp.float32
    )
    probe_projected = jnp.einsum(
        "tec,eg->tcg", column_factor_stack, probes, precision=lax.Precision.HIGHEST
    )
    sibling_nodes = []
    for level_bit in range(depth):
        own_total = probe_projected[level_bit]
        for lowest_level_flag in range(level_bit):
            own_total = own_total + partner(own_total, "leaf", lowest_level_flag)
        sibling_nodes.append(partner(own_total, "leaf", level_bit))
    applied = applied + jnp.einsum(
        "tvi,tic->vc", row_factor_stack, jnp.stack(sibling_nodes), precision=lax.Precision.HIGHEST
    )
    total_points = leaf_points * lax.axis_size("leaf")
    gathered = lax.all_gather(applied, "probe", axis=1, tiled=True)
    probe_gram = (
        lax.psum_scatter(
            jnp.dot(
                gathered.T,
                applied,
                precision=lax.Precision.HIGHEST,
                preferred_element_type=jnp.float32,
            ),
            "leaf",
            scatter_dimension=0,
            tiled=True,
        )
        / total_points
    )
    return (applied, probe_gram)


def solution(mesh):
    return jax.shard_map(
        local,
        mesh=mesh,
        in_specs=(
            P("leaf", None),
            P("leaf", None, None),
            P(None, "leaf", None),
            P(None, "leaf", None),
            P("leaf", "probe"),
        ),
        out_specs=(P("leaf", "probe"), P("leaf", "probe")),
        check_vma=False,
    )
```

profile of v0, /device:TPU:3, one launch (start us, length us, event | category | flops | bytes accessed | tf_op | source)
XLA Modules:
  0.0 162.7 jit_solution(1617433805427100048)
XLA Ops:
  7.2 0.0 copy-start
  7.2 0.0 copy-start.1
  7.2 0.0 copy-start.3
  7.2 0.0 all-gather.2.cloned.1.call-start
  7.2 0.0 copy-start.2
  7.3 4.5 %fusion.3 = f32[3,128,256]{2,1,0:T(8,128)S(1)} fusion(f32[3,1024,128]{2,1,0:T(8,128)} %param.8, f32[1024,256]{1,0:T(8,128)} %param.9), kind=kOutput, calls=%fused_computation.5 | convolution fusion | flops 1207959552 | bytes 3014656 | tf_op jit(solution)/shard_map/tec,eg->tcg/dot_general | solution.py:26
  11.8 0.7 collective-permute-start.3
  12.5 0.1 collective-permute-start.1
  12.6 0.4 collective-permute-start
  13.0 0.5 collective-permute-done.3
  13.5 0.4 collective-permute-done.1
  13.9 0.1 collective-permute-start.4
  14.0 0.0 copy-done.3
  14.0 1.4 collective-permute-start.2
  15.4 3.4 %collective-permute-done.4 = f32[128,256]{1,0:T(8,128)S(1)} collective-permute-done((f32[128,256]{1,0:T(8,128)S(1)}, f32[128,256]{1,0:T(8,128)S(1)}, u32[]{:S(2)}, u32[]{:S(2)}) %collective-permute-start.4) | collective-permute-done | bytes 131104 | tf_op jit(solution)/shard_map/ppermute | solution.py:10
  18.8 1.3 collective-permute-start.5
  20.1 0.3 mul.11
  20.5 0.0 copy-done.1
  20.5 0.0 copy-done.2
  20.5 3.6 %fusion = f32[1024,256]{1,0:T(8,128)S(1)} fusion(f32[1024,256]{1,0:T(8,128)S(1)} %copy-done.1, f32[1024,1024]{1,0:T(8,128)S(1)} %copy-done.2, f32[128,8,8,128]{3,2,1,0:T(8,128)S(1)} %bitcast.34), kind=kOutput, calls=%fused_computation.1 | convolution fusion | flops 3222274048 | bytes 10485760 | tf_op jit(solution)/shard_map/dot_general | solution.py:23
  24.2 0.0 collective-permute-done
  24.2 0.0 collective-permute-done.2
  24.2 0.0 collective-permute-done.5
  24.2 0.0 copy-done
  24.2 2.9 %fusion.2 = f32[1024,256]{1,0:T(8,128)} fusion(f32[1024,256]{1,0:T(8,128)S(1)} %fusion, f32[3,1024,128]{2,1,0:T(8,128)S(1)} %copy-done, f32[1,128,256]{2,1,0:T(8,128)S(1)} %bitcast.37, f32[1,128,256]{2,1,0:T(8,128)S(1)} %bitcast.36, f32[1,128,256]{2,1,0:T(8,128)S(1)} %bitcast.35), kind=kOutput, calls=%fused_computation.4 | convolution fusion | flops 1208418304 | bytes 4063232 | tf_op jit(solution)/shard_map/tvi,tic->vc/dot_general | solution.py:35
  27.1 0.0 all-gather.2.cloned.1.call-update
  27.1 0.2 reduce-scatter.2.cloned.1.call-start
  27.3 82.4 %all-gather.2.cloned.1.call-done = f32[1024,1024]{1,0:T(8,128)} async-done(((f32[1024,256]{1,0:T(8,128)}), f32[1024,1024]{1,0:T(8,128)}) %all-gather.2.cloned.1.call-update) | async-done | bytes 4194320 | tf_op jit(solution)/shard_map/all_gather | solution.py:39
  109.8 10.1 %fusion.13 = f32[1024,256]{1,0:T(8,128)} fusion(f32[1024,1024]{1,0:T(8,128)} %all-gather.2.cloned.1.call-done, f32[1024,256]{1,0:T(8,128)} %fusion.2), kind=kOutput, calls=%fused_computation.20 | convolution fusion | flops 3221225472 | bytes 6291456 | tf_op jit(solution)/shard_map/dot_general | solution.py:42
  119.9 0.0 reduce-scatter.2.cloned.1.call-update
  119.9 34.4 %reduce-scatter.2.cloned.1.call-done = f32[128,256]{1,0:T(8,128)} async-done(((f32[1024,256]{1,0:T(8,128)}), f32[128,256]{1,0:T(8,128)}) %reduce-scatter.2.cloned.1.call-update) | async-done | bytes 131088 | tf_op jit(solution)/shard_map/reduce_scatter | solution.py:41
  154.3 1.6 broadcast_multiply_fusion
  (4 shorter events, 0.1 us)
Async XLA Ops:
  7.2 17.0 %copy-start = (f32[3,1024,128]{2,1,0:T(8,128)S(1)}, f32[3,1024,128]{2,1,0:T(8,128)}, u32[]{:S(2)}) copy-start(f32[3,1024,128]{2,1,0:T(8,128)} %param.7) | copy-start | bytes 4718596
  7.2 13.3 %copy-start.1 = (f32[1024,256]{1,0:T(8,128)S(1)}, f32[1024,256]{1,0:T(8,128)}, u32[]{:S(2)}) copy-start(f32[1024,256]{1,0:T(8,128)} %param.9) | copy-start | bytes 3145732
  7.2 6.8 %copy-start.3 = (s32[1,8,8]{2,1,0:T(8,128)S(1)}, s32[1,8,8]{2,1,0:T(8,128)}, u32[]{:S(2)}) copy-start(s32[1,8,8]{2,1,0:T(8,128)} %param.6) | copy-start | bytes 772
  7.2 102.6 %all-gather.2.cloned.1.call-start = ((), (), s32[]{:S(2)}) async-start(), calls=%async_computation.1 | async-start | bytes 5242880 | tf_op jit(solution)/shard_map/all_gather | solution.py:39
  7.2 13.3 %copy-start.2 = (f32[1024,1024]{1,0:T(8,128)S(1)}, f32[1024,1024]{1,0:T(8,128)}, u32[]{:S(2)}) copy-start(f32[1024,1024]{1,0:T(8,128)} %param.5) | copy-start | bytes 12582916
  11.8 1.7 %collective-permute-start.3 = (f32[128,256]{1,0:T(8,128)S(1)}, f32[128,256]{1,0:T(8,128)S(1)}, u32[]{:S(2)}, u32[]{:S(2)}) collective-permute-start(f32[128,256]{1,0:T(8,128)S(1)} %get-tuple-element.3), channel_id=1, source_target_pairs={{0,4},{4,0},{8,12},{12,8},{16,20},{20,16},{24,28},{28,24},{1,5},{5... | collective-permute-start | bytes 393224 | tf_op jit(solution)/shard_map/ppermute | solution.py:10
  12.5 1.3 collective-permute-start.1
  12.6 11.6 %collective-permute-start = (f32[128,256]{1,0:T(8,128)S(1)}, f32[128,256]{1,0:T(8,128)S(1)}, u32[]{:S(2)}, u32[]{:S(2)}) collective-permute-start(f32[128,256]{1,0:T(8,128)S(1)} %get-tuple-element.2), channel_id=1, source_target_pairs={{0,4},{4,0},{8,12},{12,8},{16,20},{20,16},{24,28},{28,24},{1,5},{5... | collective-permute-start | bytes 393224 | tf_op jit(solution)/shard_map/ppermute | solution.py:10
  13.9 4.9 %collective-permute-start.4 = (f32[128,256]{1,0:T(8,128)S(1)}, f32[128,256]{1,0:T(8,128)S(1)}, u32[]{:S(2)}, u32[]{:S(2)}) collective-permute-start(f32[128,256]{1,0:T(8,128)S(1)} %get-tuple-element.6), channel_id=1, source_target_pairs={{0,8},{4,12},{8,0},{12,4},{16,24},{20,28},{24,16},{28,20},{1,9},{5... | collective-permute-start | bytes 393224 | tf_op jit(solution)/shard_map/ppermute | solution.py:10
  14.0 10.2 %collective-permute-start.2 = (f32[128,256]{1,0:T(8,128)S(1)}, f32[128,256]{1,0:T(8,128)S(1)}, u32[]{:S(2)}, u32[]{:S(2)}) collective-permute-start(f32[128,256]{1,0:T(8,128)S(1)} %get-tuple-element.5), channel_id=1, source_target_pairs={{0,8},{4,12},{8,0},{12,4},{16,24},{20,28},{24,16},{28,20},{1,9},{5... | collective-permute-start | bytes 393224 | tf_op jit(solution)/shard_map/ppermute | solution.py:10
  18.8 5.3 %collective-permute-start.5 = (f32[128,256]{1,0:T(8,128)S(1)}, f32[128,256]{1,0:T(8,128)S(1)}, u32[]{:S(2)}, u32[]{:S(2)}) collective-permute-start(f32[128,256]{1,0:T(8,128)S(1)} %add.16), channel_id=1, source_target_pairs={{0,16},{4,20},{8,24},{12,28},{16,0},{20,4},{24,8},{28,12},{1,17},{... | collective-permute-start | bytes 393224 | tf_op jit(solution)/shard_map/ppermute | solution.py:10
  27.1 127.2 %reduce-scatter.2.cloned.1.call-start = ((), (), s32[]{:S(2)}) async-start(), calls=%async_computation.2 | async-start | bytes 1179648 | tf_op jit(solution)/shard_map/reduce_scatter | solution.py:41
Sparse Core Ops, SparseCore 0:
  27.2 82.4 all-gather.1
  120.0 34.2 reduce-scatter.1
where the time goes:
time: 165 us; the launch traced here: 163 us
  waiting for transfers between devices  121 us (73%)
  matrix products  21.1 us (13%)
  between operations  14.2 us (9%)
  starting transfers between devices  4.32 us (3%)
    all_gather x1, waiting for transfers between devices, local(): gathered = lax.all_gather(applied, 'probe', axis=1, tiled=True)  82.4 us
    reduce_scatter x1, waiting for transfers between devices, local(): lax.psum_scatter(jnp.dot(gathered.T, applied, precision=lax.Precision.HIG...  34.4 us
    dot_general x1, matrix products, local(): jnp.dot(gathered.T, applied, precision=lax.Precision.HIGHEST, preferred_e...  10.1 us
    dot_general x1, matrix products, local(): jnp.einsum('tec,eg->tcg', column_factor_stack, probes, precision=lax.Prec...  4.46 us
    ppermute x6, waiting for transfers between devices, partner(): return lax.ppermute(value, axis, pairs)  4.24 us
    ppermute x6, starting transfers between devices, partner(): return lax.ppermute(value, axis, pairs)  4.06 us
    dot_general x1, matrix products, local(): jnp.dot(masked, probes, precision=lax.Precision.HIGHEST, preferred_elemen...  3.64 us
  transfers between devices with their start and end apart: 8, of which 5 were waited for; matrix products, arithmetic and copies ran while one was open for 2% of the time, Pallas kernels for 0%

commit v1 on v0

v1 whole, which is shorter than its diff:
```python
import functools

import jax
import jax.numpy as jnp
from jax import lax
from jax.experimental import pallas as pl
from jax.experimental.pallas import tpu as pltpu
from jax.sharding import PartitionSpec as P

MESH = pl.DeviceIdType.MESH
CONTRACT_ROWS = (((0,), (0,)), ((), ()))
PLAIN = (((1,), (0,)), ((), ()))


def split(value):
    high = value.astype(jnp.bfloat16)
    return high, (value - high.astype(jnp.float32)).astype(jnp.bfloat16)


def dot3(left, right, dims):
    (lh, ll), (rh, rl) = left, right
    dot = functools.partial(lax.dot_general, dimension_numbers=dims, preferred_element_type=jnp.float32)
    return dot(lh, rh) + (dot(lh, rl) + dot(ll, rh))


def kernel(
    n_leaf, n_probe, pieces,
    mask, block_hbm, row_hbm, col_hbm, probe_hbm, app_hbm, gram_ref,
    block, row, col, probe, probe_h, probe_l, own, swap, sib_h, sib_l,
    app, app_h, app_l, got, part, shares, total, extra, turned,
    load_sem, out_sem, swap_send, swap_recv, right_send, right_recv, left_send, left_recv,
    share_send, share_recv, extra_send, extra_recv,
):
    depth, rank = row.shape[0], row.shape[2]
    points, width = app.shape
    side = mask.shape[1]
    span = points // side
    half = points // 2
    piece = half // pieces
    leaf, z = lax.axis_index("leaf"), lax.axis_index("probe")
    slab = n_probe * width // n_leaf
    fan = n_leaf // n_probe
    a, b = leaf // fan, leaf % fan
    last = n_probe - 1
    ends = n_probe > 2

    loads = [
        pltpu.make_async_copy(source, target, load_sem.at[i])
        for i, (source, target) in enumerate(
            ((probe_hbm, probe), (col_hbm, col), (block_hbm, block), (row_hbm, row))
        )
    ]
    for load in loads:
        load.start()

    barrier = pltpu.get_barrier_semaphore()

    @pl.loop(1, n_leaf)
    def _(k):
        pl.semaphore_signal(
            barrier, inc=1, device_id={"leaf": (leaf + k) % n_leaf, "probe": z}, device_id_type=MESH
        )

    @pl.when(z > 0)
    def _():
        pl.semaphore_signal(barrier, inc=1, device_id={"leaf": leaf, "probe": z - 1}, device_id_type=MESH)

    @pl.when(z < last)
    def _():
        pl.semaphore_signal(barrier, inc=1, device_id={"leaf": leaf, "probe": z + 1}, device_id_type=MESH)

    @pl.when(a != z)
    def _():
        @pl.loop(0, fan)
        def _(c):
            pl.semaphore_signal(
                barrier, inc=1, device_id={"leaf": z * fan + c, "probe": a}, device_id_type=MESH
            )

    loads[0].wait()
    ph, plo = split(probe[...])
    probe_h[...] = ph
    probe_l[...] = plo
    loads[1].wait()
    for level in range(depth):
        own[level] = dot3(split(col[level]), (probe_h[...], probe_l[...]), CONTRACT_ROWS)

    peers = n_leaf - 1 + jnp.where(z > 0, 1, 0) + jnp.where(z < last, 1, 0) + jnp.where(a != z, fan, 0)
    pl.semaphore_wait(barrier, peers)

    def exchange(step):
        away = 2**step
        other = leaf + (1 - 2 * ((leaf // away) % 2)) * away
        start = sum(depth - s for s in range(step))
        return start, pltpu.make_async_remote_copy(
            src_ref=own.at[pl.ds(step, depth - step)],
            dst_ref=swap.at[pl.ds(start, depth - step)],
            send_sem=swap_send.at[step],
            recv_sem=swap_recv.at[step],
            device_id={"leaf": other, "probe": z},
            device_id_type=MESH,
        )

    def near(i):
        rows = pl.ds(pl.multiple_of(i * span, span), span)
        strips = [
            block[rows, j * span : (j + 1) * span] * mask[0, i, j].astype(jnp.float32) for j in range(side)
        ]
        app[rows, :] = dot3(
            split(jnp.concatenate(strips, axis=1)), (probe_h[...], probe_l[...]), PLAIN
        )

    done = 0
    for step in range(depth):
        start, copy = exchange(step)
        copy.start()
        if step == 0:
            loads[2].wait()
        until = side * (step + 1) // depth

        @pl.loop(done, until)
        def _(i):
            near(i)

        done = until
        copy.wait()
        sib_h[step * rank : (step + 1) * rank, :], sib_l[step * rank : (step + 1) * rank, :] = split(
            swap[start]
        )
        for level in range(step + 1, depth):
            own[level] = own[level] + swap[start + level - step]

    def ship(source, to, slot, begin, send, recv):
        rows = pl.ds(pl.multiple_of(begin, piece), piece)
        return pltpu.make_async_remote_copy(
            src_ref=source.at[rows] if source is app else source.at[slot, rows],
            dst_ref=got.at[slot, rows],
            send_sem=send.at[slot, begin // piece],
            recv_sem=recv.at[slot, begin // piece],
            device_id={"leaf": leaf, "probe": to},
            device_id_type=MESH,
        )

    def rightward(source, slot, begin):
        return ship(source, jnp.minimum(z + 1, last), slot, begin, right_send, right_recv)

    def leftward(source, slot, begin):
        return ship(source, jnp.maximum(z - 1, 0), slot, begin, left_send, left_recv)

    loads[3].wait()
    sends_right = (z < last - 1) if ends else (z < last)
    sends_left = (z > 1) if ends else (z > 0)

    def far(begin):
        rows = pl.ds(pl.multiple_of(begin, piece), piece)
        factors = jnp.concatenate([row[level, rows, :] for level in range(depth)], axis=1)
        value = app[rows, :] + dot3(split(factors), (sib_h[...], sib_l[...]), PLAIN)
        app[rows, :] = value
        app_h[rows, :], app_l[rows, :] = split(value)

    @pl.loop(0, pieces)
    def _(c):
        up, low = c * piece, half + c * piece
        far(up)

        @pl.when(sends_right)
        def _():
            rightward(app, z, up).start()

        far(low)

        @pl.when(sends_left)
        def _():
            leftward(app, z, low).start()

    if ends:
        @pl.loop(0, pieces)
        def _(c):
            @pl.when(z == 0)
            def _():
                rightward(app, z, half + c * piece).start()

            @pl.when(z == last)
            def _():
                leftward(app, z, c * piece).start()

    keep = pltpu.make_async_copy(app, app_hbm, out_sem)
    keep.start()

    def gram(slot, source, begin, fresh):
        into = pl.ds(pl.multiple_of(slot * width, width), width)
        rows = pl.ds(pl.multiple_of(begin, half), half)
        here = (app_h[rows, :], app_l[rows, :])
        there = here if source is None else split(source[slot, rows, :])
        value = dot3(there, here, CONTRACT_ROWS)
        part[into, :] = value if fresh else part[into, :] + value

    part[...] = jnp.zeros_like(part)

    @pl.loop(0, 2)
    def _(h):
        gram(z, None, h * half, False)

    @pl.loop(1, n_probe)
    def _(d):
        from_left = (z - d >= 0) & ((z < last) | (d > 1) | (not ends))
        from_right = (z + d <= last) & ((z > 0) | (d > 1) | (not ends))
        low_slot, high_slot = jnp.maximum(z - d, 0), jnp.minimum(z + d, last)

        @pl.loop(0, pieces)
        def _(c):
            up, low = c * piece, half + c * piece

            @pl.when(from_left)
            def _():
                rightward(got, low_slot, up).wait_recv()

                @pl.when(z < last)
                def _():
                    rightward(got, low_slot, up).start()

            @pl.when(from_right)
            def _():
                leftward(got, high_slot, low).wait_recv()

                @pl.when(z > 0)
                def _():
                    leftward(got, high_slot, low).start()

        @pl.loop(0, 2)
        def _(h):
            @pl.when(jnp.where(h == 0, from_left, from_right))
            def _():
                gram(jnp.where(h == 0, low_slot, high_slot), got, h * half, False)

    if ends:
        at_low, at_high = z == 1, z == last - 1

        @pl.loop(0, pieces)
        def _(c):
            @pl.when(at_low)
            def _():
                rightward(got, z - 1, half + c * piece).wait_recv()

            @pl.when(at_high)
            def _():
                leftward(got, z + 1, c * piece).wait_recv()

        @pl.loop(0, 2)
        def _(h):
            @pl.when(jnp.where(h == 0, at_high, at_low))
            def _():
                gram(jnp.where(h == 0, jnp.minimum(z + 1, last), jnp.maximum(z - 1, 0)), got, h * half, False)

    def share(k):
        to = (leaf + k) % n_leaf
        return pltpu.make_async_remote_copy(
            src_ref=part.at[pl.ds(pl.multiple_of(to * slab, slab), slab)],
            dst_ref=shares.at[k],
            send_sem=share_send.at[k],
            recv_sem=share_recv.at[k],
            device_id={"leaf": to, "probe": z},
            device_id_type=MESH,
        )

    @pl.loop(1, n_leaf)
    def _(k):
        share(k).start()

    total[...] = part[pl.ds(pl.multiple_of(leaf * slab, slab), slab), :]

    @pl.loop(1, n_leaf)
    def _(k):
        share(k).wait_recv()
        total[...] = total[...] + shares[k]

    scale = 1.0 / (points * n_leaf)

    def trade(c):
        return pltpu.make_async_remote_copy(
            src_ref=total,
            dst_ref=extra.at[pl.ds(pl.multiple_of(b * slab, slab), slab)],
            send_sem=extra_send.at[c],
            recv_sem=extra_recv.at[b],
            device_id={"leaf": z * fan + c, "probe": a},
            device_id_type=MESH,
        )

    def traded(c):
        return pltpu.make_async_remote_copy(
            src_ref=total,
            dst_ref=extra.at[pl.ds(pl.multiple_of(c * slab, slab), slab)],
            send_sem=extra_send.at[c],
            recv_sem=extra_recv.at[c],
            device_id={"leaf": z * fan + c, "probe": a},
            device_id_type=MESH,
        )

    @pl.when(a != z)
    def _():
        @pl.loop(0, fan)
        def _(c):
            trade(c).start()

        @pl.loop(0, fan)
        def _(c):
            traded(c).wait_recv()

        turned[...] = extra[...].T
        gram_ref[...] = (total[...] + turned[pl.ds(pl.multiple_of(b * slab, slab), slab), :]) * scale

        @pl.loop(0, fan)
        def _(c):
            trade(c).wait_send()

    @pl.when(a == z)
    def _():
        gram_ref[...] = total[...] * scale

    @pl.loop(0, pieces)
    def _(c):
        up, low = c * piece, half + c * piece

        @pl.when(sends_right)
        def _():
            rightward(app, z, up).wait_send()

        @pl.when(sends_left)
        def _():
            leftward(app, z, low).wait_send()

        if ends:

            @pl.when(z == 0)
            def _():
                rightward(app, z, low).wait_send()

            @pl.when(z == last)
            def _():
                leftward(app, z, up).wait_send()

        @pl.loop(1, n_probe)
        def _(d):
            @pl.when((z - d >= 0) & (z < last))
            def _():
                rightward(got, jnp.maximum(z - d, 0), up).wait_send()

            @pl.when((z + d <= last) & (z > 0))
            def _():
                leftward(got, jnp.minimum(z + d, last), low).wait_send()

    @pl.loop(1, n_leaf)
    def _(k):
        share(k).wait_send()

    keep.wait()


def local(n_leaf, n_probe, leaf_blocks, block_mask, row_factor_stack, column_factor_stack, probes):
    depth, points, rank = row_factor_stack.shape
    width = probes.shape[1]
    slab = n_probe * width // n_leaf
    fan = n_leaf // n_probe
    pieces = 4
    f32, bf16 = jnp.float32, jnp.bfloat16
    dma = pltpu.SemaphoreType.DMA
    hbm = pl.BlockSpec(memory_space=pl.ANY)
    return pl.pallas_call(
        functools.partial(kernel, n_leaf, n_probe, pieces),
        out_shape=(
            jax.ShapeDtypeStruct((points, width), f32),
            jax.ShapeDtypeStruct((slab, width), f32),
        ),
        in_specs=[pl.BlockSpec(memory_space=pltpu.SMEM), hbm, hbm, hbm, hbm],
        out_specs=(hbm, pl.BlockSpec(memory_space=pltpu.VMEM)),
        scratch_shapes=[
            pltpu.VMEM((points, points), f32),
            pltpu.VMEM((depth, points, rank), f32),
            pltpu.VMEM((depth, points, rank), f32),
            pltpu.VMEM((points, width), f32),
            pltpu.VMEM((points, width), bf16),
            pltpu.VMEM((points, width), bf16),
            pltpu.VMEM((depth, rank, width), f32),
            pltpu.VMEM((depth * (depth + 1) // 2, rank, width), f32),
            pltpu.VMEM((depth * rank, width), bf16),
            pltpu.VMEM((depth * rank, width), bf16),
            pltpu.VMEM((points, width), f32),
            pltpu.VMEM((points, width), bf16),
            pltpu.VMEM((points, width), bf16),
            pltpu.VMEM((n_probe, points, width), f32),
            pltpu.VMEM((n_probe * width, width), f32),
            pltpu.VMEM((n_leaf, slab, width), f32),
            pltpu.VMEM((slab, width), f32),
            pltpu.VMEM((width, width), f32),
            pltpu.VMEM((width, width), f32),
            dma((4,)),
            dma,
            dma((depth,)),
            dma((depth,)),
            dma((n_probe, 2 * pieces)),
            dma((n_probe, 2 * pieces)),
            dma((n_probe, 2 * pieces)),
            dma((n_probe, 2 * pieces)),
            dma((n_leaf,)),
            dma((n_leaf,)),
            dma((fan,)),
            dma((fan,)),
        ],
        compiler_params=pltpu.CompilerParams(
            collective_id=0, has_side_effects=True, vmem_limit_bytes=48 * 2**20
        ),
    )(block_mask, leaf_blocks, row_factor_stack, column_factor_stack, probes)


def solution(mesh):
    return jax.shard_map(
        functools.partial(local, mesh.shape["leaf"], mesh.shape["probe"]),
        mesh=mesh,
        in_specs=(
            P("leaf", None),
            P("leaf", None, None),
            P(None, "leaf", None),
            P(None, "leaf", None),
            P("leaf", "probe"),
        ),
        out_specs=(P("leaf", "probe"), P("leaf", "probe")),
        check_vma=False,
    )
```

time: 165 us -> 82.3 us (0.50); the launches traced: 163 us -> 82.1 us
  waiting for transfers between devices: 121 us -> 0 us
  Pallas kernels: 0 us -> 75.1 us
  matrix products: 21.1 us -> 0 us
  between operations: 14.2 us -> 0.65 us
  local copies, waits for them, and re-layouts: 0.38 us -> 6.35 us
  starting transfers between devices: 4.32 us -> 0 us
    all_gather x1 -> x0, waiting for transfers between devices: 82.4 us -> none  [local(): gathered = lax.all_gather(applied, 'probe', axis=1, tiled=True)]
    pallas_call x0 -> x1, Pallas kernels: none -> 75.1 us  [local(): pl.pallas_call(functools.partial(kernel, n_leaf, n_probe, pieces), out_sh...]
    reduce_scatter x1 -> x0, waiting for transfers between devices: 34.4 us -> none  [local(): lax.psum_scatter(jnp.dot(gathered.T, applied, precision=lax.Precision.HIG...]
    dot_general x4 -> x0, matrix products: 21.1 us -> none  [the longest x1 10.1 us: local(): jnp.dot(gathered.T, applied, precision=lax.Precision.HIGHEST, preferred_e...]
    unnamed x8 -> x10, local copies, waits for them, and re-layouts: 0.02 us -> 6.35 us
    ppermute x6 -> x0, waiting for transfers between devices: 4.24 us -> none  [partner(): return lax.ppermute(value, axis, pairs)]
    ppermute x6 -> x0, starting transfers between devices: 4.06 us -> none  [partner(): return lax.ppermute(value, axis, pairs)]
  transfers between devices with their start and end apart: 8 -> 0, of which waited for: 5 -> 0; matrix products, arithmetic and copies ran while one was open for 2% -> 0% of each run, Pallas kernels for 0% -> 0%
where the time goes in v1:
time: 82.3 us; the launch traced here: 82.1 us
  Pallas kernels  75.1 us (91%)
  local copies, waits for them, and re-layouts  6.35 us (8%)
    pallas_call x1, Pallas kernels, local(): pl.pallas_call(functools.partial(kernel, n_leaf, n_probe, pieces), out_sh...  75.1 us
    unnamed x10, local copies, waits for them, and re-layouts  6.35 us

profile of v1, /device:TPU:3, one launch (start us, length us, event | category | flops | bytes accessed | tf_op | source)
XLA Modules:
  0.0 82.1 jit_solution(4053571164357927903)
XLA Ops:
  0.6 0.0 copy-start
  0.6 1.4 %copy-done = f32[3,1024,128]{2,1,0:T(8,128)S(1)} copy-done((f32[3,1024,128]{2,1,0:T(8,128)S(1)}, f32[3,1024,128]{2,1,0:T(8,128)}, u32[]{:S(2)}) %copy-start) | copy-done | bytes 1572888
  2.0 0.0 copy-start.1
  2.0 1.4 %copy-done.1 = f32[3,1024,128]{2,1,0:T(8,128)S(1)} copy-done((f32[3,1024,128]{2,1,0:T(8,128)S(1)}, f32[3,1024,128]{2,1,0:T(8,128)}, u32[]{:S(2)}) %copy-start.1) | copy-done | bytes 1572888
  3.4 0.0 copy-start.2
  3.5 1.2 %copy-done.2 = f32[1024,256]{1,0:T(8,128)S(1)} copy-done((f32[1024,256]{1,0:T(8,128)S(1)}, f32[1024,256]{1,0:T(8,128)}, u32[]{:S(2)}) %copy-start.2) | copy-done | bytes 1048600
  4.7 0.0 copy-start.3
  4.7 0.7 copy-done.3
  5.4 75.1 %shard_map.68 = (f32[1024,256]{1,0:T(8,128)S(1)}, f32[128,256]{1,0:T(8,128)S(1)}) custom-call(s32[1,8,8]{2,1,0:T(8,128)S(1)} %copy-done.3, f32[1024,1024]{1,0:T(8,128)} %block_hbm.1, f32[3,1024,128]{2,1,0:T(8,128)S(1)} %copy-done, f32[3,1024,128]{2,1,0:T(8,128)S(1)} %copy-done.1, f32[1024,256]{1,0:T(8,128)S(1)} %copy-done.2), custom_call_target="tpu_custom_call" | custom-call | tf_op jit(solution)/shard_map/pallas_call | solution.py:368
  80.4 1.0 %copy.9 = f32[1024,256]{1,0:T(8,128)} copy(f32[1024,256]{1,0:T(8,128)S(1)} %get-tuple-element.4) | data formatting | bytes 2097152
  81.4 0.7 copy.10
Async XLA Ops:
  0.6 1.4 %copy-start = (f32[3,1024,128]{2,1,0:T(8,128)S(1)}, f32[3,1024,128]{2,1,0:T(8,128)}, u32[]{:S(2)}) copy-start(f32[3,1024,128]{2,1,0:T(8,128)} %row_hbm.1) | copy-start | bytes 4718596
  2.0 1.4 %copy-start.1 = (f32[3,1024,128]{2,1,0:T(8,128)S(1)}, f32[3,1024,128]{2,1,0:T(8,128)}, u32[]{:S(2)}) copy-start(f32[3,1024,128]{2,1,0:T(8,128)} %col_hbm.1) | copy-start | bytes 4718596
  3.4 1.2 %copy-start.2 = (f32[1024,256]{1,0:T(8,128)S(1)}, f32[1024,256]{1,0:T(8,128)}, u32[]{:S(2)}) copy-start(f32[1024,256]{1,0:T(8,128)} %probe_hbm.1) | copy-start | bytes 3145732
  4.7 0.7 copy-start.3

commit v2 on v1

--- a/solution.py
+++ b/solution.py
@@ -27,7 +27,7 @@
     n_leaf, n_probe, pieces,
     mask, block_hbm, row_hbm, col_hbm, probe_hbm, app_hbm, gram_ref,
     block, row, col, probe, probe_h, probe_l, own, swap, sib_h, sib_l,
-    app, app_h, app_l, got, part, shares, total, extra, turned,
+    app, app_h, app_l, got, part, shares, total, extra, turned, kept_h, kept_l,
     load_sem, out_sem, swap_send, swap_recv, right_send, right_recv, left_send, left_recv,
     share_send, share_recv, extra_send, extra_recv,
 ):
@@ -82,8 +82,8 @@
     probe_h[...] = ph
     probe_l[...] = plo
     loads[1].wait()
-    for level in range(depth):
-        own[level] = dot3(split(col[level]), (probe_h[...], probe_l[...]), CONTRACT_ROWS)
+    columns = jnp.concatenate([col[level] for level in range(depth)], axis=1)
+    own[...] = dot3(split(columns), (probe_h[...], probe_l[...]), CONTRACT_ROWS).reshape(own.shape)
 
     peers = n_leaf - 1 + jnp.where(z > 0, 1, 0) + jnp.where(z < last, 1, 0) + jnp.where(a != z, fan, 0)
     pl.semaphore_wait(barrier, peers)
@@ -101,28 +101,30 @@
             device_id_type=MESH,
         )
 
-    def near(i):
-        rows = pl.ds(pl.multiple_of(i * span, span), span)
-        strips = [
-            block[rows, j * span : (j + 1) * span] * mask[0, i, j].astype(jnp.float32) for j in range(side)
-        ]
-        app[rows, :] = dot3(
-            split(jnp.concatenate(strips, axis=1)), (probe_h[...], probe_l[...]), PLAIN
-        )
-
-    done = 0
+    def near(which):
+        @pl.loop(0, side // 2)
+        def _(i):
+            line = which * (side // 2) + i
+            rows = pl.ds(pl.multiple_of(line * span, span), span)
+            strips = [
+                block[rows, j * span : (j + 1) * span] * mask[0, line, j].astype(jnp.float32)
+                for j in range(side)
+            ]
+            into = pl.ds(pl.multiple_of(i * span, span), span)
+            kept_h[into, :], kept_l[into, :] = split(jnp.concatenate(strips, axis=1))
+
+        app[which * half : (which + 1) * half, :] = dot3(
+            (kept_h[...], kept_l[...]), (probe_h[...], probe_l[...]), PLAIN
+        )
+
     for step in range(depth):
         start, copy = exchange(step)
         copy.start()
         if step == 0:
             loads[2].wait()
-        until = side * (step + 1) // depth
-
-        @pl.loop(done, until)
-        def _(i):
-            near(i)
-
-        done = until
+        for which in range(2):
+            if step == min(which, depth - 1):
+                near(which)
         copy.wait()
         sib_h[step * rank : (step + 1) * rank, :], sib_l[step * rank : (step + 1) * rank, :] = split(
             swap[start]
@@ -151,27 +153,28 @@
     sends_right = (z < last - 1) if ends else (z < last)
     sends_left = (z > 1) if ends else (z > 0)
 
-    def far(begin):
-        rows = pl.ds(pl.multiple_of(begin, piece), piece)
+    def far(which):
+        rows = slice(which * half, (which + 1) * half)
         factors = jnp.concatenate([row[level, rows, :] for level in range(depth)], axis=1)
         value = app[rows, :] + dot3(split(factors), (sib_h[...], sib_l[...]), PLAIN)
         app[rows, :] = value
         app_h[rows, :], app_l[rows, :] = split(value)
 
-    @pl.loop(0, pieces)
-    def _(c):
-        up, low = c * piece, half + c * piece
-        far(up)
-
-        @pl.when(sends_right)
-        def _():
-            rightward(app, z, up).start()
-
-        far(low)
-
-        @pl.when(sends_left)
-        def _():
-            leftward(app, z, low).start()
+    far(0)
+
+    @pl.when(sends_right)
+    def _():
+        @pl.loop(0, pieces)
+        def _(c):
+            rightward(app, z, c * piece).start()
+
+    far(1)
+
+    @pl.when(sends_left)
+    def _():
+        @pl.loop(0, pieces)
+        def _(c):
+            leftward(app, z, half + c * piece).start()
 
     if ends:
         @pl.loop(0, pieces)
@@ -194,63 +197,6 @@
         there = here if source is None else split(source[slot, rows, :])
         value = dot3(there, here, CONTRACT_ROWS)
         part[into, :] = value if fresh else part[into, :] + value
-
-    part[...] = jnp.zeros_like(part)
-
-    @pl.loop(0, 2)
-    def _(h):
-        gram(z, None, h * half, False)
-
-    @pl.loop(1, n_probe)
-    def _(d):
-        from_left = (z - d >= 0) & ((z < last) | (d > 1) | (not ends))
-        from_right = (z + d <= last) & ((z > 0) | (d > 1) | (not ends))
-        low_slot, high_slot = jnp.maximum(z - d, 0), jnp.minimum(z + d, last)
-
-        @pl.loop(0, pieces)
-        def _(c):
-            up, low = c * piece, half + c * piece
-
-            @pl.when(from_left)
-            def _():
-                rightward(got, low_slot, up).wait_recv()
-
-                @pl.when(z < last)
-                def _():
-                    rightward(got, low_slot, up).start()
-
-            @pl.when(from_right)
-            def _():
-                leftward(got, high_slot, low).wait_recv()
-
-                @pl.when(z > 0)
-                def _():
-                    leftward(got, high_slot, low).start()
-
-        @pl.loop(0, 2)
-        def _(h):
-            @pl.when(jnp.where(h == 0, from_left, from_right))
-            def _():
-                gram(jnp.where(h == 0, low_slot, high_slot), got, h * half, False)
-
-    if ends:
-        at_low, at_high = z == 1, z == last - 1
-
-        @pl.loop(0, pieces)
-        def _(c):
-            @pl.when(at_low)
-            def _():
-                rightward(got, z - 1, half + c * piece).wait_recv()
-
-            @pl.when(at_high)
-            def _():
-                leftward(got, z + 1, c * piece).wait_recv()
-
-        @pl.loop(0, 2)
-        def _(h):
-            @pl.when(jnp.where(h == 0, at_high, at_low))
-            def _():
-                gram(jnp.where(h == 0, jnp.minimum(z + 1, last), jnp.maximum(z - 1, 0)), got, h * half, False)
 
     def share(k):
         to = (leaf + k) % n_leaf
@@ -263,55 +209,125 @@
             device_id_type=MESH,
         )
 
-    @pl.loop(1, n_leaf)
-    def _(k):
-        share(k).start()
+    def give(slot):
+        @pl.loop(0, fan)
+        def _(c):
+            to = slot * fan + c
+
+            @pl.when(to != leaf)
+            def _():
+                share((to - leaf + n_leaf) % n_leaf).start()
+
+    part[...] = jnp.zeros_like(part)
+
+    @pl.loop(0, 2)
+    def _(h):
+        gram(z, None, h * half, False)
+
+    give(z)
+
+    @pl.loop(1, n_probe)
+    def _(d):
+        from_left = (z - d >= 0) & ((z < last) | (d > 1) | (not ends))
+        from_right = (z + d <= last) & ((z > 0) | (d > 1) | (not ends))
+        low_slot, high_slot = jnp.maximum(z - d, 0), jnp.minimum(z + d, last)
+
+        @pl.loop(0, pieces)
+        def _(c):
+            up, low = c * piece, half + c * piece
+
+            @pl.when(from_left)
+            def _():
+                rightward(got, low_slot, up).wait_recv()
+
+                @pl.when(z < last)
+                def _():
+                    rightward(got, low_slot, up).start()
+
+            @pl.when(from_right)
+            def _():
+                leftward(got, high_slot, low).wait_recv()
+
+                @pl.when(z > 0)
+                def _():
+                    leftward(got, high_slot, low).start()
+
+        @pl.loop(0, 2)
+        def _(h):
+            @pl.when(jnp.where(h == 0, from_left, from_right))
+            def _():
+                slot = jnp.where(h == 0, low_slot, high_slot)
+                gram(slot, got, h * half, False)
+                whole = (d > 1) | jnp.where(h == 0, z != 1, z != last - 1) | (not ends)
+
+                @pl.when(whole)
+                def _():
+                    give(slot)
+
+    if ends:
+        at_low, at_high = z == 1, z == last - 1
+
+        @pl.loop(0, pieces)
+        def _(c):
+            @pl.when(at_low)
+            def _():
+                rightward(got, z - 1, half + c * piece).wait_recv()
+
+            @pl.when(at_high)
+            def _():
+                leftward(got, z + 1, c * piece).wait_recv()
+
+        @pl.loop(0, 2)
+        def _(h):
+            @pl.when(jnp.where(h == 0, at_high, at_low))
+            def _():
+                slot = jnp.where(h == 0, jnp.minimum(z + 1, last), jnp.maximum(z - 1, 0))
+                gram(slot, got, h * half, False)
+                give(slot)
 
     total[...] = part[pl.ds(pl.multiple_of(leaf * slab, slab), slab), :]
 
-    @pl.loop(1, n_leaf)
-    def _(k):
-        share(k).wait_recv()
-        total[...] = total[...] + shares[k]
+    def holds(slot):
+        return (not ends) | (((z > 0) | (slot != 1)) & ((z < last) | (slot != last - 1)))
+
+    @pl.when(holds(a))
+    def _():
+        @pl.loop(1, n_leaf)
+        def _(k):
+            share(k).wait_recv()
+            total[...] = total[...] + shares[k]
 
     scale = 1.0 / (points * n_leaf)
 
-    def trade(c):
+    tile = extra.shape[1]
+
+    def trade(c, at):
         return pltpu.make_async_remote_copy(
-            src_ref=total,
-            dst_ref=extra.at[pl.ds(pl.multiple_of(b * slab, slab), slab)],
+            src_ref=total if tile == width else total.at[:, pl.ds(pl.multiple_of(c * tile, tile), tile)],
+            dst_ref=extra.at[pl.ds(pl.multiple_of(at * slab, slab), slab)],
             send_sem=extra_send.at[c],
-            recv_sem=extra_recv.at[b],
+            recv_sem=extra_recv.at[at],
             device_id={"leaf": z * fan + c, "probe": a},
             device_id_type=MESH,
         )
 
-    def traded(c):
-        return pltpu.make_async_remote_copy(
-            src_ref=total,
-            dst_ref=extra.at[pl.ds(pl.multiple_of(c * slab, slab), slab)],
-            send_sem=extra_send.at[c],
-            recv_sem=extra_recv.at[c],
-            device_id={"leaf": z * fan + c, "probe": a},
-            device_id_type=MESH,
-        )
-
     @pl.when(a != z)
     def _():
         @pl.loop(0, fan)
         def _(c):
-            trade(c).start()
+            trade(c, b).start()
 
         @pl.loop(0, fan)
         def _(c):
-            traded(c).wait_recv()
+            trade(c, c).wait_recv()
 
         turned[...] = extra[...].T
-        gram_ref[...] = (total[...] + turned[pl.ds(pl.multiple_of(b * slab, slab), slab), :]) * scale
+        skip = 0 if tile == slab else pl.multiple_of(b * slab, slab)
+        gram_ref[...] = (total[...] + turned[pl.ds(skip, slab), :]) * scale
 
         @pl.loop(0, fan)
         def _(c):
-            trade(c).wait_send()
+            trade(c, b).wait_send()
 
     @pl.when(a == z)
     def _():
@@ -351,7 +367,9 @@
 
     @pl.loop(1, n_leaf)
     def _(k):
-        share(k).wait_send()
+        @pl.when(holds(((leaf + k) % n_leaf) // fan))
+        def _():
+            share(k).wait_send()
 
     keep.wait()
 
@@ -362,9 +380,10 @@
     slab = n_probe * width // n_leaf
     fan = n_leaf // n_probe
     pieces = 4
+    tile = slab if slab % 128 == 0 else width
     f32, bf16 = jnp.float32, jnp.bfloat16
     dma = pltpu.SemaphoreType.DMA
-    hbm = pl.BlockSpec(memory_space=pl.ANY)
+    hbm = pl.BlockSpec(memory_space=pltpu.HBM)
     return pl.pallas_call(
         functools.partial(kernel, n_leaf, n_probe, pieces),
         out_shape=(
@@ -391,8 +410,10 @@
             pltpu.VMEM((n_probe * width, width), f32),
             pltpu.VMEM((n_leaf, slab, width), f32),
             pltpu.VMEM((slab, width), f32),
-            pltpu.VMEM((width, width), f32),
-            pltpu.VMEM((width, width), f32),
+            pltpu.VMEM((width, tile), f32),
+            pltpu.VMEM((tile, width), f32),
+            pltpu.VMEM((points // 2, points), bf16),
+            pltpu.VMEM((points // 2, points), bf16),
             dma((4,)),
             dma,
             dma((depth,)),
@@ -407,7 +428,7 @@
             dma((fan,)),
         ],
         compiler_params=pltpu.CompilerParams(
-            collective_id=0, has_side_effects=True, vmem_limit_bytes=48 * 2**20
+            collective_id=0, has_side_effects=True, vmem_limit_bytes=67043328
         ),
     )(block_mask, leaf_blocks, row_factor_stack, column_factor_stack, probes)
 

time: 82.3 us -> 71.7 us (0.87)
  Pallas kernels: 75.1 us -> 67.9 us
  local copies, waits for them, and re-layouts: 6.35 us -> 2.96 us
    pallas_call x1, Pallas kernels: 75.1 us -> 67.9 us  [local(): pl.pallas_call(functools.partial(kernel, n_leaf, n_probe, pieces), out_sh...]
    unnamed x10 -> x4, local copies, waits for them, and re-layouts: 6.35 us -> 2.96 us
where the time goes in v2:
time: 71.7 us; the launch traced here: 71.5 us
  Pallas kernels  67.9 us (95%)
  local copies, waits for them, and re-layouts  2.96 us (4%)
    pallas_call x1, Pallas kernels, local(): pl.pallas_call(functools.partial(kernel, n_leaf, n_probe, pieces), out_sh...  67.9 us
    unnamed x4, local copies, waits for them, and re-layouts  2.96 us

profile of v2, /device:TPU:3, one launch (start us, length us, event | category | flops | bytes accessed | tf_op | source)
XLA Modules:
  0.0 71.5 jit_solution(9565460882202471363)
XLA Ops:
  0.6 67.9 %shard_map.68 = (f32[1024,256]{1,0:T(8,128)}, f32[128,256]{1,0:T(8,128)}) custom-call(s32[1,8,8]{2,1,0:T(8,128)} %mask.1, f32[1024,1024]{1,0:T(8,128)} %block_hbm.1, f32[3,1024,128]{2,1,0:T(8,128)} %row_hbm.1, f32[3,1024,128]{2,1,0:T(8,128)} %col_hbm.1, f32[1024,256]{1,0:T(8,128)} %probe_hbm.1), custom_call_target="tpu_custom_call" | custom-call | tf_op jit(solution)/shard_map/pallas_call | solution.py:387
  68.6 0.0 copy-start
  68.6 2.3 %copy.9 = f32[1024,256]{1,0:T(8,128)} copy(f32[1024,256]{1,0:T(8,128)} %get-tuple-element.4) | data formatting | bytes 2097152
  70.9 0.0 copy-done
  70.9 0.7 copy.10
Async XLA Ops:
  68.6 2.3 %copy-start = (f32[128,256]{1,0:T(8,128)S(1)}, f32[128,256]{1,0:T(8,128)}, u32[]{:S(2)}) copy-start(f32[128,256]{1,0:T(8,128)} %get-tuple-element.5) | copy-start | bytes 393220

commit v3 on v2

--- a/solution.py
+++ b/solution.py
@@ -26,9 +26,9 @@
 def kernel(
     n_leaf, n_probe, pieces,
     mask, block_hbm, row_hbm, col_hbm, probe_hbm, app_hbm, gram_ref,
-    block, row, col, probe, probe_h, probe_l, own, swap, sib_h, sib_l,
+    block, row, col, probe, probe_h, probe_l, own, swap, rest, sib_h, sib_l,
     app, app_h, app_l, got, part, shares, total, extra, turned, kept_h, kept_l,
-    load_sem, out_sem, swap_send, swap_recv, right_send, right_recv, left_send, left_recv,
+    load_sem, out_sem, swap_send, swap_recv, rest_send, rest_recv, right_send, right_recv, left_send, left_recv,
     share_send, share_recv, extra_send, extra_recv,
 ):
     depth, rank = row.shape[0], row.shape[2]
@@ -50,8 +50,8 @@
             ((probe_hbm, probe), (col_hbm, col), (block_hbm, block), (row_hbm, row))
         )
     ]
-    for load in loads:
-        load.start()
+    loads[0].start()
+    loads[1].start()
 
     barrier = pltpu.get_barrier_semaphore()
 
@@ -82,22 +82,40 @@
     probe_h[...] = ph
     probe_l[...] = plo
     loads[1].wait()
+    loads[2].start()
+    loads[3].start()
     columns = jnp.concatenate([col[level] for level in range(depth)], axis=1)
-    own[...] = dot3(split(columns), (probe_h[...], probe_l[...]), CONTRACT_ROWS).reshape(own.shape)
+    projected = dot3(split(columns), (probe_h[...], probe_l[...]), CONTRACT_ROWS)
+    strip = own.shape[3]
+    for side_half in range(2):
+        own[side_half] = projected[:, side_half * strip : (side_half + 1) * strip].reshape(own.shape[1:])
 
     peers = n_leaf - 1 + jnp.where(z > 0, 1, 0) + jnp.where(z < last, 1, 0) + jnp.where(a != z, fan, 0)
     pl.semaphore_wait(barrier, peers)
+
+    mine = leaf % 2
+    mate = leaf + 1 - 2 * mine
 
     def exchange(step):
         away = 2**step
         other = leaf + (1 - 2 * ((leaf // away) % 2)) * away
         start = sum(depth - s for s in range(step))
         return start, pltpu.make_async_remote_copy(
-            src_ref=own.at[pl.ds(step, depth - step)],
+            src_ref=own.at[1 - mine if step == 0 else mine, pl.ds(step, depth - step)],
             dst_ref=swap.at[pl.ds(start, depth - step)],
             send_sem=swap_send.at[step],
             recv_sem=swap_recv.at[step],
             device_id={"leaf": other, "probe": z},
+            device_id_type=MESH,
+        )
+
+    def complete(level):
+        return pltpu.make_async_remote_copy(
+            src_ref=own.at[mine, 0] if level == 0 else swap.at[sum(depth - s for s in range(level))],
+            dst_ref=rest.at[level],
+            send_sem=rest_send.at[level],
+            recv_sem=rest_recv.at[level],
+            device_id={"leaf": mate, "probe": z},
             device_id_type=MESH,
         )
 
@@ -117,20 +135,28 @@
             (kept_h[...], kept_l[...]), (probe_h[...], probe_l[...]), PLAIN
         )
 
+    def sibling(level, which, value):
+        rows, lanes = slice(level * rank, (level + 1) * rank), pl.ds(pl.multiple_of(which * strip, strip), strip)
+        sib_h[rows, lanes], sib_l[rows, lanes] = split(value)
+
     for step in range(depth):
         start, copy = exchange(step)
         copy.start()
         if step == 0:
+            complete(0).start()
             loads[2].wait()
         for which in range(2):
             if step == min(which, depth - 1):
                 near(which)
         copy.wait()
-        sib_h[step * rank : (step + 1) * rank, :], sib_l[step * rank : (step + 1) * rank, :] = split(
-            swap[start]
-        )
+        if step > 0:
+            complete(step).start()
         for level in range(step + 1, depth):
-            own[level] = own[level] + swap[start + level - step]
+            own[mine, level] = own[mine, level] + swap[start + level - step]
+        sibling(step, mine, swap[start])
+    for level in range(depth):
+        complete(level).wait()
+        sibling(level, 1 - mine, rest[level])
 
     def ship(source, to, slot, begin, send, recv):
         rows = pl.ds(pl.multiple_of(begin, piece), piece)
@@ -399,8 +425,9 @@
             pltpu.VMEM((points, width), f32),
             pltpu.VMEM((points, width), bf16),
             pltpu.VMEM((points, width), bf16),
-            pltpu.VMEM((depth, rank, width), f32),
-            pltpu.VMEM((depth * (depth + 1) // 2, rank, width), f32),
+            pltpu.VMEM((2, depth, rank, width // 2), f32),
+            pltpu.VMEM((depth * (depth + 1) // 2, rank, width // 2), f32),
+            pltpu.VMEM((depth, rank, width // 2), f32),
             pltpu.VMEM((depth * rank, width), bf16),
             pltpu.VMEM((depth * rank, width), bf16),
             pltpu.VMEM((points, width), f32),
@@ -418,6 +445,8 @@
             dma,
             dma((depth,)),
             dma((depth,)),
+            dma((depth,)),
+            dma((depth,)),
             dma((n_probe, 2 * pieces)),
             dma((n_probe, 2 * pieces)),
             dma((n_probe, 2 * pieces)),

time: 71.7 us -> 73 us (1.018)
  Pallas kernels: 67.9 us -> 69.2 us
    pallas_call x1, Pallas kernels: 67.9 us -> 69.2 us  [local(): pl.pallas_call(functools.partial(kernel, n_leaf, n_probe, pieces), out_sh...]
where the time goes in v3:
time: 73 us; the launch traced here: 72.8 us
  Pallas kernels  69.2 us (95%)
  local copies, waits for them, and re-layouts  2.96 us (4%)
    pallas_call x1, Pallas kernels, local(): pl.pallas_call(functools.partial(kernel, n_leaf, n_probe, pieces), out_sh...  69.2 us
    unnamed x4, local copies, waits for them, and re-layouts  2.96 us

profile of v3, /device:TPU:3, one launch (start us, length us, event | category | flops | bytes accessed | tf_op | source)
XLA Modules:
  0.0 72.8 jit_solution(15326924133434603277)
XLA Ops:
  0.6 69.2 %shard_map.68 = (f32[1024,256]{1,0:T(8,128)}, f32[128,256]{1,0:T(8,128)}) custom-call(s32[1,8,8]{2,1,0:T(8,128)} %mask.1, f32[1024,1024]{1,0:T(8,128)} %block_hbm.1, f32[3,1024,128]{2,1,0:T(8,128)} %row_hbm.1, f32[3,1024,128]{2,1,0:T(8,128)} %col_hbm.1, f32[1024,256]{1,0:T(8,128)} %probe_hbm.1), custom_call_target="tpu_custom_call" | custom-call | tf_op jit(solution)/shard_map/pallas_call | solution.py:413
  69.9 0.0 copy-start
  69.9 2.3 %copy.9 = f32[1024,256]{1,0:T(8,128)} copy(f32[1024,256]{1,0:T(8,128)} %get-tuple-element.4) | data formatting | bytes 2097152
  72.2 0.0 copy-done
  72.2 0.7 copy.10
Async XLA Ops:
  69.9 2.3 %copy-start = (f32[128,256]{1,0:T(8,128)S(1)}, f32[128,256]{1,0:T(8,128)}, u32[]{:S(2)}) copy-start(f32[128,256]{1,0:T(8,128)} %get-tuple-element.5) | copy-start | bytes 393220

commit v4 on v2

--- a/solution.py
+++ b/solution.py
@@ -50,8 +50,8 @@
             ((probe_hbm, probe), (col_hbm, col), (block_hbm, block), (row_hbm, row))
         )
     ]
-    for load in loads:
-        load.start()
+    loads[0].start()
+    loads[1].start()
 
     barrier = pltpu.get_barrier_semaphore()
 
@@ -82,6 +82,8 @@
     probe_h[...] = ph
     probe_l[...] = plo
     loads[1].wait()
+    loads[2].start()
+    loads[3].start()
     columns = jnp.concatenate([col[level] for level in range(depth)], axis=1)
     own[...] = dot3(split(columns), (probe_h[...], probe_l[...]), CONTRACT_ROWS).reshape(own.shape)
 

time: 71.7 us -> 70.8 us (0.987)
  Pallas kernels: 67.9 us -> 67 us
    pallas_call x1, Pallas kernels: 67.9 us -> 67 us  [local(): pl.pallas_call(functools.partial(kernel, n_leaf, n_probe, pieces), out_sh...]
where the time goes in v4:
time: 70.8 us; the launch traced here: 70.6 us
  Pallas kernels  67 us (95%)
  local copies, waits for them, and re-layouts  2.96 us (4%)
    pallas_call x1, Pallas kernels, local(): pl.pallas_call(functools.partial(kernel, n_leaf, n_probe, pieces), out_sh...  67 us
    unnamed x4, local copies, waits for them, and re-layouts  2.96 us

profile of v4, /device:TPU:3, one launch (start us, length us, event | category | flops | bytes accessed | tf_op | source)
XLA Modules:
  0.0 70.6 jit_solution(5397964439202906605)
XLA Ops:
  0.6 67.0 %shard_map.68 = (f32[1024,256]{1,0:T(8,128)}, f32[128,256]{1,0:T(8,128)}) custom-call(s32[1,8,8]{2,1,0:T(8,128)} %mask.1, f32[1024,1024]{1,0:T(8,128)} %block_hbm.1, f32[3,1024,128]{2,1,0:T(8,128)} %row_hbm.1, f32[3,1024,128]{2,1,0:T(8,128)} %col_hbm.1, f32[1024,256]{1,0:T(8,128)} %probe_hbm.1), custom_call_target="tpu_custom_call" | custom-call | tf_op jit(solution)/shard_map/pallas_call | solution.py:389
  67.6 0.0 copy-start
  67.6 2.3 %copy.9 = f32[1024,256]{1,0:T(8,128)} copy(f32[1024,256]{1,0:T(8,128)} %get-tuple-element.4) | data formatting | bytes 2097152
  69.9 0.0 copy-done
  69.9 0.7 copy.10
Async XLA Ops:
  67.6 2.3 %copy-start = (f32[128,256]{1,0:T(8,128)S(1)}, f32[128,256]{1,0:T(8,128)}, u32[]{:S(2)}) copy-start(f32[128,256]{1,0:T(8,128)} %get-tuple-element.5) | copy-start | bytes 393220
